TPU v7x, 512 devices: a whole 4x4x16 slice. The times are simulated.
512 devices in a mesh: dp: 32 (over z, y_lo), fsdp: 16 (over x, y_hi, core).
Axes of the slice: x: 4, y: 4 (y_hi: 2, y_lo: 2; y = y_hi * 2 + y_lo), z: 16, core: 2. Of those that a mesh axis runs over, the one named last changes fastest.
Arguments:
- tokens: bfloat16 [65536, 1024], P(('dp', 'fsdp')), may hold values from -6 to 6
- cotangent: bfloat16 [65536, 1024], P(('dp', 'fsdp')), may hold values from -6 to 6
- routes: int32 [65536, 1], P(('dp', 'fsdp')), may hold values from 0 to 32; in each aligned block of 128 rows (0 to 127, 128 to 255, ...) at most 4 rows name the same one
- norm_gain_vector: float32 [1024], replicated, may hold values from 0.25 to 1.75
- up_weight: bfloat16 [1024, 4096], P(None, 'fsdp'), may hold values from -0.1875 to 0.1875
- up_bias: float32 [4096], P('fsdp'), may hold values from -4 to 4
- down_weight: bfloat16 [4096, 1024], P('fsdp'), may hold values from -0.09375 to 0.09375
Outputs:
- input_grad: bfloat16 [65536, 1024], P(('dp', 'fsdp'))
- up_grad: float32 [1024, 4096], P(None, 'fsdp')
- bias_grad: float32 [4096], P('fsdp')
- down_grad: float32 [4096, 1024], P('fsdp')
- gain_grad: float32 [1024], replicated
Inputs may be any that keep to these rules, and one draw needn't show every extreme that they name: `routes`: among the 128 slots of one device no value below 32 appears more than 4 times; the value 32 marks a padding slot.
All inputs are finite; a program needn't handle non-finite values.
Results may differ from a plain program's by a relative error of at most 0.024.
Values may be sent and summed in bfloat16 or wider, within the bound.
A program may use at most 128 MiB of HBM per device.

v0:
```python
import jax
import jax.numpy as jnp
from jax import lax
from jax.sharding import Mesh
from jax.sharding import PartitionSpec as P

DP = ("dp_0", "dp_1")
FSDP = ("fsdp_0", "fsdp_1", "fsdp_2")
ROWS_AXES = ("fsdp_0", "fsdp_1")
DP_FSDP = ("dp_0", "dp_1", "fsdp_0", "fsdp_1", "fsdp_2")
root_two_pi = 0.7978845608
cubic = 0.044715


def side_by_side(arrays, axis, split_dim, concat_dim, along):
    both = jnp.concatenate(arrays, axis=along)
    filled, at, finished = (
        lax.all_to_all(both, axis, split_axis=split_dim, concat_axis=concat_dim, tiled=True),
        0,
        [],
    )
    for a in arrays:
        finished.append(lax.slice_in_dim(filled, at, at + a.shape[along], axis=along))
        at += a.shape[along]
    return tuple(finished)


def gelu_pair(pre):
    inner = root_two_pi * (pre + cubic * pre * pre * pre)
    tangent = jnp.tanh(inner)
    act = 0.5 * pre * (1.0 + tangent)
    slope = 0.5 * (1.0 + tangent) + 0.5 * pre * (1.0 - tangent * tangent) * root_two_pi * (
        1.0 + 3.0 * cubic * pre * pre
    )
    return (act, slope)


def apply_layer_norm(values):
    row_average = jnp.mean(values, axis=1, keepdims=True)
    centered = values - row_average
    variance = jnp.mean(centered * centered, axis=1, keepdims=True)
    inverse_std = 1.0 / jnp.sqrt(variance + 1e-05)
    return (centered * inverse_std, inverse_std)


def shards(tokens, cotangent, routes, norm_gain_vector, up_weight, up_bias, down_weight):
    particle_slot_count = tokens.shape[0]
    dp_size = lax.axis_size(DP)
    capacity = particle_slot_count // dp_size
    up_weight = lax.all_gather(up_weight, "fsdp_2", axis=1, tiled=True)
    down_weight = lax.all_gather(down_weight, "fsdp_2", axis=0, tiled=True)
    up_bias = lax.all_gather(up_bias, "fsdp_2", axis=0, tiled=True)
    target = routes[:, 0]
    matches = (target[:, None] == jnp.arange(dp_size + 1, dtype=jnp.int32)[None, :]).astype(
        jnp.int32
    )
    earlier = jnp.cumsum(matches, axis=0) - matches
    ranked = jnp.sum(earlier * matches, axis=1)
    slot_index = jnp.where(target < dp_size, target * capacity + ranked, -1)
    placing = (
        slot_index[None, :] == jnp.arange(particle_slot_count, dtype=jnp.int32)[:, None]
    ).astype(jnp.bfloat16)
    send_in = jnp.dot(placing, tokens, preferred_element_type=jnp.float32).astype(jnp.bfloat16)
    send_cot = jnp.dot(placing, cotangent, preferred_element_type=jnp.float32).astype(jnp.bfloat16)
    packed_in, packed_cot = side_by_side((send_in, send_cot), DP, 0, 0, 1)
    local_standardized, own_inverse = apply_layer_norm(packed_in.astype(jnp.float32))
    normed_local = (local_standardized * norm_gain_vector).astype(jnp.bfloat16)
    all_cot = lax.all_gather(packed_cot, ROWS_AXES, axis=0, tiled=True)
    gathered_normed_rows = lax.all_gather(normed_local, ROWS_AXES, axis=0, tiled=True)
    pre = jnp.dot(gathered_normed_rows, up_weight, preferred_element_type=jnp.float32) + up_bias
    act_full, slope = gelu_pair(pre)
    act = act_full.astype(jnp.bfloat16)
    act_grad = jnp.einsum("rd,kd->rk", all_cot, down_weight, preferred_element_type=jnp.float32)
    pre_grad = (act_grad * slope).astype(jnp.bfloat16)
    down_part = jnp.einsum("rk,rd->kd", act, all_cot, preferred_element_type=jnp.float32)
    up_part = jnp.einsum(
        "rk,rd->kd", pre_grad, gathered_normed_rows, preferred_element_type=jnp.float32
    )
    bias_part = jnp.sum(pre_grad.astype(jnp.float32), axis=0)
    partial_gain_grad = (
        jnp.sum(up_part * up_weight.T.astype(jnp.float32), axis=0) / norm_gain_vector
    )
    parts = jnp.concatenate([up_part, down_part], axis=1).astype(jnp.bfloat16)
    mine = lax.psum_scatter(parts, "fsdp_2", scatter_dimension=0, tiled=True)
    mine = lax.psum_scatter(mine, DP, scatter_dimension=0, tiled=True)
    whole = lax.all_gather(mine, DP, axis=0, tiled=True).astype(jnp.float32)
    d = up_weight.shape[0]
    up_grad = whole[:, :d].T
    down_grad = whole[:, d:]
    normed_rows_gradient = lax.psum_scatter(
        jnp.einsum("rk,dk->rd", pre_grad, up_weight, preferred_element_type=jnp.float32).astype(
            jnp.bfloat16
        ),
        ROWS_AXES,
        scatter_dimension=0,
        tiled=True,
    ).astype(jnp.float32)
    index = lax.axis_index(FSDP)
    k = bias_part.shape[0] // 2
    wide = jnp.zeros((8, 2 * k), jnp.float32)
    wide = lax.dynamic_update_slice(wide, bias_part[None], (index // 2, 0))
    small = lax.psum(jnp.concatenate([partial_gain_grad, wide.reshape(-1)]), DP_FSDP)
    gain_grad = small[:d]
    bias_grad = lax.dynamic_slice(small[d:], (index * k,), (k,))
    scaled_values = normed_rows_gradient * norm_gain_vector
    final_result = packed_cot.astype(jnp.float32) + own_inverse * (
        scaled_values
        - jnp.mean(scaled_values, axis=1, keepdims=True)
        - local_standardized * jnp.mean(scaled_values * local_standardized, axis=1, keepdims=True)
    )
    return (final_result.astype(jnp.bfloat16), up_grad, bias_grad, down_grad, gain_grad)


def solution(mesh):
    finer = Mesh(
        mesh.devices.reshape(16, 2, 4, 2, 2), ("dp_0", "dp_1", "fsdp_0", "fsdp_1", "fsdp_2")
    )
    return jax.shard_map(
        shards,
        mesh=finer,
        in_specs=(
            P(DP_FSDP, None),
            P(DP_FSDP, None),
            P(DP_FSDP, None),
            P(),
            P(None, FSDP),
            P(FSDP),
            P(FSDP, None),
        ),
        out_specs=(P(DP_FSDP, None), P(None, FSDP), P(FSDP), P(FSDP, None), P()),
        check_vma=False,
    )
```

profile of v0, /device:TPU:2, one launch (start us, length us, event | category | flops | bytes accessed | tf_op | source)
XLA Modules:
  0.0 631.0 jit_solution(15258363506738329338)
XLA Ops:
  9.9 1.2 convolution_convert_fusion.3
  11.1 1.0 all_to_all.8
  12.1 16.6 %all-to-all-start = ((bf16[32,4,2048]{2,1,0:T(4,128)(2,1)}), bf16[32,4,2048]{2,1,0:T(4,128)(2,1)S(1)}, u32[]{:S(2)}, u32[]{:S(2)}) async-start(bf16[32,4,2048]{2,1,0:T(4,128)(2,1)} %all_to_all.8), calls=%async_computation | async-start | bytes 1048576 | tf_op jit(solution)/shard_map/all_to_all | solution.py:18
  28.8 1.0 copy.14
  29.9 31.9 %all-to-all-done = bf16[32,4,2048]{2,1,0:T(4,128)(2,1)S(1)} async-done(((bf16[32,4,2048]{2,1,0:T(4,128)(2,1)}), bf16[32,4,2048]{2,1,0:T(4,128)(2,1)S(1)}, u32[]{:S(2)}, u32[]{:S(2)}) %all-to-all-start) | async-done | bytes 524320 | tf_op jit(solution)/shard_map/all_to_all | solution.py:18
  64.6 1.8 all-gather
  66.4 61.5 %all-gather.11.cloned.1.call-done = bf16[1024,1024]{1,0:T(8,128)(2,1)} async-done(((bf16[128,1024]{1,0:T(8,128)(2,1)}), bf16[1024,1024]{1,0:T(8,128)(2,1)}) %all-gather.11.cloned.1.call-update) | async-done | bytes 2097168 | tf_op jit(solution)/shard_map/all_gather | solution.py:69
  127.9 4.4 fusion.33
  132.4 68.8 %all-gather.7.cloned.1.call-done = bf16[1024,1024]{1,0:T(8,128)(2,1)} async-done(((bf16[128,1024]{1,0:T(8,128)(2,1)}), bf16[1024,1024]{1,0:T(8,128)(2,1)}) %all-gather.7.cloned.1.call-update) | async-done | bytes 2097168 | tf_op jit(solution)/shard_map/all_gather | solution.py:68
  201.1 3.6 convolution_convert_fusion.1
  204.8 17.0 %all-gather.9.cloned.1.call-done = bf16[512,1024]{1,0:T(8,128)(2,1)} async-done(((bf16[256,1024]{1,0:T(8,128)(2,1)}), bf16[512,1024]{1,0:T(8,128)(2,1)}) %all-gather.9.cloned.1.call-update) | async-done | bytes 1048592 | tf_op jit(solution)/shard_map/all_gather | solution.py:51
  221.8 5.1 convert_reduce_fusion
  226.9 1.3 fusion.7
  228.2 1.5 pad_maximum_fusion
  229.8 21.8 %reduce-scatter.6.cloned.1.call-done = bf16[256,2048]{1,0:T(8,128)(2,1)} async-done(((bf16[512,2048]{1,0:T(8,128)(2,1)}), bf16[256,2048]{1,0:T(8,128)(2,1)}) %reduce-scatter.6.cloned.1.call-update) | async-done | bytes 1048592 | tf_op jit(solution)/shard_map/reduce_scatter | solution.py:84
  251.6 2.6 convolution_convert_fusion
  254.3 139.2 %reduce-scatter.8.cloned.1.call-done = bf16[8,2048]{1,0:T(8,128)(2,1)} async-done(((bf16[256,2048]{1,0:T(8,128)(2,1)}), bf16[8,2048]{1,0:T(8,128)(2,1)}) %reduce-scatter.8.cloned.1.call-update) | async-done | bytes 32784 | tf_op jit(solution)/shard_map/reduce_scatter | solution.py:85
  393.7 100.6 %psum.7 = f32[5120]{0:T(1024)S(1)} all-reduce(f32[5120]{0:T(1024)S(1)} %pad_maximum_fusion.2), channel_id=1, replica_groups=mesh['dp_0'=16,'dp_1'=2,'fsdp_0'=4,'fsdp_1'=2,'fsdp_2'=2] {'dp_0','dp_1'..., use_global_device_ids=true, to_apply=%region_11.12 | all-reduce | flops 5120 | bytes 40960 | tf_op jit(solution)/shard_map/psum | solution.py:102
  495.5 1.2 fusion.25
  496.7 1.9 fusion.23
  498.6 121.5 %all-gather.15.cloned.1.call-done = bf16[256,2048]{1,0:T(8,128)(2,1)} async-done(((bf16[8,2048]{1,0:T(8,128)(2,1)}), bf16[256,2048]{1,0:T(8,128)(2,1)}) %all-gather.15.cloned.1.call-update) | async-done | bytes 1048592 | tf_op jit(solution)/shard_map/all_gather | solution.py:86
  620.1 1.5 convert_element_type.58
  621.7 1.3 copy.15
  623.0 1.1 slice.28
  (59 shorter events, 7.2 us)
Async XLA Ops:
  7.2 2.5 copy-start
  9.6 19.1 %copy-start.2 = (bf16[1024,256]{1,0:T(8,128)(2,1)S(1)}, bf16[1024,256]{1,0:T(8,128)(2,1)}, u32[]{:S(2)}) copy-start(bf16[1024,256]{1,0:T(8,128)(2,1)} %param.11) | copy-start | bytes 1572868
  12.1 50.1 %copy-start.3 = (f32[1024]{0:T(1024)S(1)}, f32[1024]{0:T(1024)}, u32[]{:S(2)}) copy-start(f32[1024]{0:T(1024)} %param.10) | copy-start | bytes 12292
  12.1 49.7 %all-to-all-start = ((bf16[32,4,2048]{2,1,0:T(4,128)(2,1)}), bf16[32,4,2048]{2,1,0:T(4,128)(2,1)S(1)}, u32[]{:S(2)}, u32[]{:S(2)}) async-start(bf16[32,4,2048]{2,1,0:T(4,128)(2,1)} %all_to_all.8), calls=%async_computation | async-start | bytes 1048576 | tf_op jit(solution)/shard_map/all_to_all | solution.py:18
  28.7 37.7 %all-gather.13.cloned.1.call-start = ((), (), s32[]{:S(2)}) async-start(), calls=%async_computation.7 | async-start | bytes 1572864 | tf_op jit(solution)/shard_map/all_gather | solution.py:50
  29.8 34.8 %copy-start.4 = (f32[256]{0:T(256)S(1)}, f32[256]{0:T(256)}, u32[]{:S(2)}) copy-start(f32[256]{0:T(256)} %param.12) | copy-start | bytes 3076
  29.8 98.1 %all-gather.11.cloned.1.call-start = ((), (), s32[]{:S(2)}) async-start(), calls=%async_computation.6 | async-start | bytes 2359296 | tf_op jit(solution)/shard_map/all_gather | solution.py:69
  63.2 138.0 %all-gather.7.cloned.1.call-start = ((), (), s32[]{:S(2)}) async-start(), calls=%async_computation.4 | async-start | bytes 2359296 | tf_op jit(solution)/shard_map/all_gather | solution.py:68
  64.0 157.8 %all-gather.9.cloned.1.call-start = ((), (), s32[]{:S(2)}) async-start(), calls=%async_computation.5 | async-start | bytes 1572864 | tf_op jit(solution)/shard_map/all_gather | solution.py:51
  64.5 187.0 %reduce-scatter.6.cloned.1.call-start = ((), (), s32[]{:S(2)}) async-start(), calls=%async_computation.9 | async-start | bytes 3145728 | tf_op jit(solution)/shard_map/reduce_scatter | solution.py:84
  204.7 22.2 %copy-start.6 = (bf16[1024,512]{0,1:T(8,128)(2,1)S(1)}, bf16[1024,512]{0,1:T(8,128)(2,1)}, u32[]{:S(2)}) copy-start(bf16[1024,512]{0,1:T(8,128)(2,1)} %all-gather.13.cloned.1.call-done) | copy-start | bytes 3145732
  221.8 5.1 copy-start.5
  226.9 1.3 copy-start.7
  229.7 21.9 %copy-start.8 = (bf16[1024,512]{1,0:T(8,128)(2,1)S(1)}, bf16[1024,512]{1,0:T(8,128)(2,1)}, u32[]{:S(2)}) copy-start(bf16[1024,512]{1,0:T(8,128)(2,1)} %copy-done.7) | copy-start | bytes 3145732
  229.7 163.8 %reduce-scatter.8.cloned.1.call-start = ((), (), s32[]{:S(2)}) async-start(), calls=%async_computation.10 | async-start | bytes 1081344 | tf_op jit(solution)/shard_map/reduce_scatter | solution.py:85
  251.6 243.9 %reduce-scatter.4.cloned.1.call-start = ((), (), s32[]{:S(2)}) async-start(), calls=%async_computation.8 | async-start | bytes 2359296 | tf_op jit(solution)/shard_map/reduce_scatter | solution.py:90
  254.3 365.9 %all-gather.15.cloned.1.call-start = ((), (), s32[]{:S(2)}) async-start(), calls=%async_computation.11 | async-start | bytes 1081344 | tf_op jit(solution)/shard_map/all_gather | solution.py:86
  621.6 1.4 copy-start.1
Sparse Core Ops, SparseCore 0:
  32.2 20.3 all-gather.12
  63.3 64.5 all-gather.10
  131.7 69.3 all-gather.6
  203.1 18.6 all-gather.8
  229.9 21.6 reduce-scatter.5
  254.2 139.2 reduce-scatter.7
  398.2 89.2 reduce-scatter.3
  489.5 130.5 all-gather.14
where the time goes:
time: 631 us
  waiting for transfers between devices  462 us (73%)
  blocking collectives  102 us (16%)
  matrix products  18.4 us (3%)
  starting transfers between devices  17 us (3%)
  between operations  14.4 us (2%)
  other arithmetic  9.85 us (2%)
  local copies, waits for them, and re-layouts  6.69 us (1%)
    reduce_scatter x1, waiting for transfers between devices, shards(): mine = lax.psum_scatter(mine, DP, scatter_dimension=0, tiled=True)  139 us
    all_gather x1, waiting for transfers between devices, shards(): whole = lax.all_gather(mine, DP, axis=0, tiled=True).astype(jnp.float32)  122 us
    psum x1, blocking collectives, shards(): lax.psum(jnp.concatenate([partial_gain_grad, wide.reshape(-1)]), DP_FSDP)  101 us
    all_gather x1, waiting for transfers between devices, shards(): all_cot = lax.all_gather(packed_cot, ROWS_AXES, axis=0, tiled=True)  68.8 us
    all_gather x1, waiting for transfers between devices, shards(): lax.all_gather(normed_local, ROWS_AXES, axis=0, tiled=True)  61.5 us
    all_to_all x1, waiting for transfers between devices, side_by_side(): lax.all_to_all(both, axis, split_axis=split_dim, concat_axis=concat_dim,...  31.9 us
    reduce_scatter x1, waiting for transfers between devices, shards(): mine = lax.psum_scatter(parts, 'fsdp_2', scatter_dimension=0, tiled=True)  21.8 us
    all_gather x1, waiting for transfers between devices, shards(): down_weight = lax.all_gather(down_weight, 'fsdp_2', axis=0, tiled=True)  17 us
  transfers between devices with their start and end apart: 9, of which 7 were waited for; matrix products, arithmetic and copies ran while one was open for 3% of the time, Pallas kernels for 0%

commit v1 on v0

--- a/solution.py
+++ b/solution.py
@@ -83,7 +83,9 @@
     parts = jnp.concatenate([up_part, down_part], axis=1).astype(jnp.bfloat16)
     mine = lax.psum_scatter(parts, "fsdp_2", scatter_dimension=0, tiled=True)
     mine = lax.psum_scatter(mine, DP, scatter_dimension=0, tiled=True)
-    whole = lax.all_gather(mine, DP, axis=0, tiled=True).astype(jnp.float32)
+    whole = jnp.concatenate(
+        lax.all_to_all(jnp.stack([mine] * lax.axis_size(DP)), DP, 0, 0), axis=0
+    ).astype(jnp.float32)
     d = up_weight.shape[0]
     up_grad = whole[:, :d].T
     down_grad = whole[:, d:]

time: 631 us -> 528 us (0.84)
  the two profiles are of different devices: /device:TPU:2 before, /device:TPU:1 now
where the time goes in v1:
time: 528 us
  waiting for transfers between devices  315 us (60%)
  blocking collectives  137 us (26%)
  starting transfers between devices  26.2 us (5%)
  matrix products  18.5 us (4%)
  between operations  14.4 us (3%)
  other arithmetic  8.66 us (2%)
  local copies, waits for them, and re-layouts  8.49 us (2%)
    psum x1, blocking collectives, shards(): lax.psum(jnp.concatenate([partial_gain_grad, wide.reshape(-1)]), DP_FSDP)  132 us
    reduce_scatter x1, waiting for transfers between devices, shards(): mine = lax.psum_scatter(mine, DP, scatter_dimension=0, tiled=True)  114 us
    all_gather x1, waiting for transfers between devices, shards(): all_cot = lax.all_gather(packed_cot, ROWS_AXES, axis=0, tiled=True)  68.8 us
    all_gather x1, waiting for transfers between devices, shards(): lax.all_gather(normed_local, ROWS_AXES, axis=0, tiled=True)  59.9 us
    all_to_all x1, waiting for transfers between devices, side_by_side(): lax.all_to_all(both, axis, split_axis=split_dim, concat_axis=concat_dim,...  30.2 us
    reduce_scatter x1, waiting for transfers between devices, shards(): mine = lax.psum_scatter(parts, 'fsdp_2', scatter_dimension=0, tiled=True)  21.2 us
    all_gather x1, waiting for transfers between devices, shards(): down_weight = lax.all_gather(down_weight, 'fsdp_2', axis=0, tiled=True)  19.7 us
    all_to_all x1, starting transfers between devices, side_by_side(): lax.all_to_all(both, axis, split_axis=split_dim, concat_axis=concat_dim,...  17.2 us
  transfers between devices with their start and end apart: 9, of which 6 were waited for; matrix products, arithmetic and copies ran while one was open for 4% of the time, Pallas kernels for 0%

profile of v1, /device:TPU:1, one launch (start us, length us, event | category | flops | bytes accessed | tf_op | source)
XLA Modules:
  0.0 527.6 jit_solution(5952640362095758041)
XLA Ops:
  9.9 1.2 convolution_convert_fusion.3
  11.1 1.0 all_to_all.11
  12.1 17.2 %all-to-all-start = ((bf16[32,4,2048]{2,1,0:T(4,128)(2,1)}), bf16[32,4,2048]{2,1,0:T(4,128)(2,1)S(1)}, u32[]{:S(2)}, u32[]{:S(2)}) async-start(bf16[32,4,2048]{2,1,0:T(4,128)(2,1)} %all_to_all.11), calls=%async_computation | async-start | bytes 1048576 | tf_op jit(solution)/shard_map/all_to_all | solution.py:18
  29.3 1.0 copy.14
  30.4 30.2 %all-to-all-done = bf16[32,4,2048]{2,1,0:T(4,128)(2,1)S(1)} async-done(((bf16[32,4,2048]{2,1,0:T(4,128)(2,1)}), bf16[32,4,2048]{2,1,0:T(4,128)(2,1)S(1)}, u32[]{:S(2)}, u32[]{:S(2)}) %all-to-all-start) | async-done | bytes 524320 | tf_op jit(solution)/shard_map/all_to_all | solution.py:18
  63.5 4.1 all-gather
  67.6 59.9 %all-gather.10.cloned.1.call-done = bf16[1024,1024]{1,0:T(8,128)(2,1)} async-done(((bf16[128,1024]{1,0:T(8,128)(2,1)}), bf16[1024,1024]{1,0:T(8,128)(2,1)}) %all-gather.10.cloned.1.call-update) | async-done | bytes 2097168 | tf_op jit(solution)/shard_map/all_gather | solution.py:69
  127.5 4.5 fusion.34
  132.0 68.8 %all-gather.6.cloned.1.call-done = bf16[1024,1024]{1,0:T(8,128)(2,1)} async-done(((bf16[128,1024]{1,0:T(8,128)(2,1)}), bf16[1024,1024]{1,0:T(8,128)(2,1)}) %all-gather.6.cloned.1.call-update) | async-done | bytes 2097168 | tf_op jit(solution)/shard_map/all_gather | solution.py:68
  200.7 3.6 convolution_convert_fusion.1
  204.3 19.7 %all-gather.8.cloned.1.call-done = bf16[512,1024]{1,0:T(8,128)(2,1)} async-done(((bf16[256,1024]{1,0:T(8,128)(2,1)}), bf16[512,1024]{1,0:T(8,128)(2,1)}) %all-gather.8.cloned.1.call-update) | async-done | bytes 1048592 | tf_op jit(solution)/shard_map/all_gather | solution.py:51
  224.1 5.1 convert_reduce_fusion
  229.2 1.3 fusion.7
  230.5 1.5 pad_maximum_fusion
  232.1 21.2 %reduce-scatter.6.cloned.1.call-done = bf16[256,2048]{1,0:T(8,128)(2,1)} async-done(((bf16[512,2048]{1,0:T(8,128)(2,1)}), bf16[256,2048]{1,0:T(8,128)(2,1)}) %reduce-scatter.6.cloned.1.call-update) | async-done | bytes 1048592 | tf_op jit(solution)/shard_map/reduce_scatter | solution.py:84
  253.4 2.6 convolution_convert_fusion
  256.0 114.5 %reduce-scatter.8.cloned.1.call-done = bf16[8,2048]{1,0:T(8,128)(2,1)} async-done(((bf16[256,2048]{1,0:T(8,128)(2,1)}), bf16[8,2048]{1,0:T(8,128)(2,1)}) %reduce-scatter.8.cloned.1.call-update) | async-done | bytes 32784 | tf_op jit(solution)/shard_map/reduce_scatter | solution.py:85
  370.5 1.8 stack.2
  372.4 8.7 %all-to-all-start.1 = ((bf16[32,8,2048]{2,1,0:T(8,128)(2,1)}), bf16[32,8,2048]{2,1,0:T(8,128)(2,1)S(1)}, u32[]{:S(2)}, u32[]{:S(2)}) async-start(bf16[32,8,2048]{2,1,0:T(8,128)(2,1)} %stack.2), calls=%async_computation.4 | async-start | bytes 2097152 | tf_op jit(solution)/shard_map/all_to_all | solution.py:87
  381.2 132.4 %psum.7 = f32[5120]{0:T(1024)S(1)} all-reduce(f32[5120]{0:T(1024)S(1)} %pad_maximum_fusion.2), channel_id=1, replica_groups=mesh['dp_0'=16,'dp_1'=2,'fsdp_0'=4,'fsdp_1'=2,'fsdp_2'=2] {'dp_0','dp_1'..., use_global_device_ids=true, to_apply=%region_11.12 | all-reduce | flops 5120 | bytes 40960 | tf_op jit(solution)/shard_map/psum | solution.py:104
  514.9 1.2 fusion.25
  516.1 1.9 fusion.23
  518.3 1.2 fusion.33
  519.4 1.3 copy.15
  (56 shorter events, 7.3 us)
Async XLA Ops:
  7.2 2.5 copy-start
  9.6 19.7 %copy-start.1 = (bf16[1024,256]{1,0:T(8,128)(2,1)S(1)}, bf16[1024,256]{1,0:T(8,128)(2,1)}, u32[]{:S(2)}) copy-start(bf16[1024,256]{1,0:T(8,128)(2,1)} %param.11) | copy-start | bytes 1572868
  12.1 49.0 %copy-start.2 = (f32[1024]{0:T(1024)S(1)}, f32[1024]{0:T(1024)}, u32[]{:S(2)}) copy-start(f32[1024]{0:T(1024)} %param.10) | copy-start | bytes 12292
  12.1 48.5 %all-to-all-start = ((bf16[32,4,2048]{2,1,0:T(4,128)(2,1)}), bf16[32,4,2048]{2,1,0:T(4,128)(2,1)S(1)}, u32[]{:S(2)}, u32[]{:S(2)}) async-start(bf16[32,4,2048]{2,1,0:T(4,128)(2,1)} %all_to_all.11), calls=%async_computation | async-start | bytes 1048576 | tf_op jit(solution)/shard_map/all_to_all | solution.py:18
  29.2 38.3 %all-gather.12.cloned.1.call-start = ((), (), s32[]{:S(2)}) async-start(), calls=%async_computation.8 | async-start | bytes 1572864 | tf_op jit(solution)/shard_map/all_gather | solution.py:50
  30.3 33.1 %copy-start.3 = (f32[256]{0:T(256)S(1)}, f32[256]{0:T(256)}, u32[]{:S(2)}) copy-start(f32[256]{0:T(256)} %param.12) | copy-start | bytes 3076
  30.3 97.2 %all-gather.10.cloned.1.call-start = ((), (), s32[]{:S(2)}) async-start(), calls=%async_computation.7 | async-start | bytes 2359296 | tf_op jit(solution)/shard_map/all_gather | solution.py:69
  62.0 138.7 %all-gather.6.cloned.1.call-start = ((), (), s32[]{:S(2)}) async-start(), calls=%async_computation.5 | async-start | bytes 2359296 | tf_op jit(solution)/shard_map/all_gather | solution.py:68
  62.8 161.2 %all-gather.8.cloned.1.call-start = ((), (), s32[]{:S(2)}) async-start(), calls=%async_computation.6 | async-start | bytes 1572864 | tf_op jit(solution)/shard_map/all_gather | solution.py:51
  63.4 189.9 %reduce-scatter.6.cloned.1.call-start = ((), (), s32[]{:S(2)}) async-start(), calls=%async_computation.10 | async-start | bytes 3145728 | tf_op jit(solution)/shard_map/reduce_scatter | solution.py:84
  204.3 24.9 %copy-start.5 = (bf16[1024,512]{0,1:T(8,128)(2,1)S(1)}, bf16[1024,512]{0,1:T(8,128)(2,1)}, u32[]{:S(2)}) copy-start(bf16[1024,512]{0,1:T(8,128)(2,1)} %all-gather.12.cloned.1.call-done) | copy-start | bytes 3145732
  224.1 5.1 copy-start.4
  229.2 1.3 copy-start.6
  232.0 21.4 %copy-start.7 = (bf16[1024,512]{1,0:T(8,128)(2,1)S(1)}, bf16[1024,512]{1,0:T(8,128)(2,1)}, u32[]{:S(2)}) copy-start(bf16[1024,512]{1,0:T(8,128)(2,1)} %copy-done.6) | copy-start | bytes 3145732
  232.1 138.4 %reduce-scatter.8.cloned.1.call-start = ((), (), s32[]{:S(2)}) async-start(), calls=%async_computation.11 | async-start | bytes 1081344 | tf_op jit(solution)/shard_map/reduce_scatter | solution.py:85
  253.4 261.5 %reduce-scatter.4.cloned.1.call-start = ((), (), s32[]{:S(2)}) async-start(), calls=%async_computation.9 | async-start | bytes 2359296 | tf_op jit(solution)/shard_map/reduce_scatter | solution.py:92
  372.4 145.7 %all-to-all-start.1 = ((bf16[32,8,2048]{2,1,0:T(8,128)(2,1)}), bf16[32,8,2048]{2,1,0:T(8,128)(2,1)S(1)}, u32[]{:S(2)}, u32[]{:S(2)}) async-start(bf16[32,8,2048]{2,1,0:T(8,128)(2,1)} %stack.2), calls=%async_computation.4 | async-start | bytes 2097152 | tf_op jit(solution)/shard_map/all_to_all | solution.py:87
Sparse Core Ops, SparseCore 0:
  32.7 22.0 all-gather.11
  62.2 65.2 all-gather.9
  131.3 69.3 all-gather.5
  202.7 21.3 all-gather.7
  232.2 21.0 reduce-scatter.5
  256.0 114.4 reduce-scatter.7
  375.1 115.9 reduce-scatter.3
